TPU v7x, 32 devices: a whole 2x2x4 slice. The times are simulated.
32 devices in a mesh: chain: 8 (over z, y), col: 4 (over x, core).
Axes of the slice: x: 2, y: 2, z: 4, core: 2. Of those that a mesh axis runs over, the one named last changes fastest.
Arguments:
- rhs: bfloat16 [4, 8, 32, 128], P(None, 'chain'), may hold values from -6 to 6
- pattern: int32 [4, 8, 24], P(None, 'chain', 'col'), may hold values from 0 to 31, as said below
- factor: bfloat16 [4, 8, 24, 128, 128], P(None, 'chain', 'col'), may hold values from -0.1875 to 0.1875
- inverse: bfloat16 [4, 8, 128, 128], P(None, 'chain'), as said below
- level_size: int32 [6], replicated, may hold values from 1 to 8, 32 in all
Outputs:
- half_solved: bfloat16 [4, 8, 32, 128], P(None, 'chain')
- solved: bfloat16 [4, 8, 32, 128], P(None, 'chain')
Inputs may be any that keep to these rules, and one draw needn't show every extreme that they name: Among the pattern entries held by one index of chain and one index of col (all 4 of its block rows), at most 3 name block rows on any one index of chain (block row mod 8); in every such group exactly 3 name block rows on one index of chain that is common to all groups of that index of col. A block row may name a block row more than once. `inverse`: each block is lower triangular with a diagonal between 0.3 and 2.
All inputs are finite; a program needn't handle non-finite values.
Results may differ from a plain program's by a relative error of at most 0.013.
Values may be sent and summed in bfloat16 or wider, within the bound.
A program may use at most 64 MiB of HBM per device.

v0:
```python
import jax
import jax.numpy as jnp
from jax import lax
from jax.sharding import PartitionSpec as P


def level_index(positions, ends):
    return jnp.sum((positions[..., None] >= ends).astype(jnp.int32), axis=-1)


def per_device(rhs, pattern, factor, inverse, level_size):
    lane_count = lax.axis_size("chain")
    chain_pos = lax.axis_index("chain")
    row_count = rhs.shape[0]
    probe_count = rhs.shape[2]
    width = rhs.shape[3]
    entries = pattern.shape[2]
    level_count = level_size.shape[0]
    total = row_count * lane_count
    ends = jnp.cumsum(level_size)
    starts = ends - level_size
    own_rows = jnp.arange(row_count, dtype=jnp.int32) * lane_count + chain_pos
    own_level = level_index(own_rows, ends)
    columns = pattern[:, 0, :]
    column_level = level_index(columns, ends)
    keep = column_level < own_level[:, None]
    blocks = factor[:, 0]
    inverse_rows = inverse[:, 0]
    right = rhs[:, 0]
    slot_ids = jnp.arange(row_count, dtype=jnp.int32)
    lane_ids = jnp.arange(lane_count, dtype=jnp.int32)

    def locate(level):
        picked = own_level == level
        own_slot = jnp.sum(jnp.where(picked, slot_ids, 0))
        return (picked, own_slot, jnp.any(picked))

    def forward_level(level, carry):
        store, half_local = carry
        picked, own_slot, is_live = locate(level)
        wanted = keep[own_slot] & is_live
        chosen = jnp.where(
            wanted[:, None, None], store[columns[own_slot]], jnp.zeros((), jnp.bfloat16)
        )
        partial_value = jnp.einsum(
            "jpb,jcb->pc", chosen, blocks[own_slot], preferred_element_type=jnp.float32
        )
        summed = lax.psum(partial_value, "col")
        rest = (right[own_slot].astype(jnp.float32) - summed).astype(jnp.bfloat16)
        segment = jnp.dot(
            rest, inverse_rows[own_slot].T, preferred_element_type=jnp.float32
        ).astype(jnp.bfloat16)
        segment = jnp.where(is_live, segment, jnp.zeros((), jnp.bfloat16))
        front = lax.all_gather(segment[None], "chain", axis=0, tiled=True)
        half_local = jnp.where(picked[:, None, None], segment[None], half_local)
        start = starts[level]
        ordered = front[(start + lane_ids) % lane_count]
        store = lax.dynamic_update_slice_in_dim(store, ordered, start, 0)
        return (store, half_local)

    store = jnp.zeros((total + lane_count, probe_count, width), jnp.bfloat16)
    half_local = jnp.zeros((row_count, probe_count, width), jnp.bfloat16)
    store, half_local = lax.fori_loop(0, level_count, forward_level, (store, half_local))
    solved_local = jnp.zeros((row_count, probe_count, width), jnp.bfloat16)
    count = row_count * entries
    capacity = max(2, (count + lane_count - 1) // lane_count)
    slots_all = lane_count * capacity
    flat_cols = columns.reshape(count)
    flat_src = jnp.broadcast_to(own_rows[:, None], (row_count, entries)).reshape(count)
    dest = flat_cols % lane_count
    onehot = (dest[:, None] == lane_ids[None, :]).astype(jnp.int32)
    before = jnp.cumsum(onehot, axis=0) - onehot
    rank = jnp.sum(before * onehot, axis=1)
    slot = dest * capacity + rank
    select = slot[None, :] == jnp.arange(slots_all, dtype=jnp.int32)[:, None]
    sent_blocks = jnp.dot(
        select.astype(jnp.bfloat16),
        blocks.reshape(count, width * width),
        preferred_element_type=jnp.float32,
    )
    sent_blocks = sent_blocks.astype(jnp.bfloat16).reshape(lane_count, capacity, width, width)
    sent_src = jnp.sum(jnp.where(select, flat_src[None, :] + 1, 0), axis=1) - 1
    sent_dst = jnp.sum(jnp.where(select, flat_cols[None, :] + 1, 0), axis=1) - 1
    sent_meta = jnp.stack([sent_src, sent_dst], axis=1).reshape(lane_count, capacity, 2)
    home_blocks, home_meta = (
        lax.all_to_all(sent_blocks, "chain", split_axis=0, concat_axis=0, tiled=True),
        lax.all_to_all(sent_meta, "chain", split_axis=0, concat_axis=0, tiled=True),
    )
    home_blocks = home_blocks.reshape(slots_all, width, width)
    home_meta = home_meta.reshape(slots_all, 2)
    source_row = home_meta[:, 0]
    target_row = home_meta[:, 1]
    valid = source_row >= 0
    source_level = level_index(source_row, ends)
    target_level = level_index(target_row, ends)
    home_keep = valid & (target_level < source_level)
    source_lane = jnp.where(valid, source_row % lane_count, 0)
    home_slot = jnp.where(valid, target_row // lane_count, -1)

    def home_level(counter, carry):
        accum, solved_now = carry
        level = level_count - 1 - counter
        picked, own_slot, is_live = locate(level)
        summed = lax.psum(accum[own_slot], "col")
        rest = (half_local[own_slot].astype(jnp.float32) - summed).astype(jnp.bfloat16)
        segment = jnp.dot(rest, inverse_rows[own_slot], preferred_element_type=jnp.float32).astype(
            jnp.bfloat16
        )
        segment = jnp.where(is_live, segment, jnp.zeros((), jnp.bfloat16))
        solved_now = jnp.where(picked[:, None, None], segment[None], solved_now)
        front = lax.all_gather(segment[None], "chain", axis=0, tiled=True)
        active = home_keep & (source_level == level)
        incoming = front[source_lane]
        terms = jnp.einsum(
            "kpc,kcb->kpb", incoming, home_blocks, preferred_element_type=jnp.float32
        )
        spread = ((home_slot[None, :] == slot_ids[:, None]) & active[None, :]).astype(jnp.float32)
        added = jnp.dot(
            spread,
            terms.reshape(slots_all, probe_count * width),
            precision=lax.Precision.HIGHEST,
            preferred_element_type=jnp.float32,
        )
        accum = accum + added.reshape(row_count, probe_count, width)
        return (accum, solved_now)

    accum = jnp.zeros((row_count, probe_count, width), jnp.float32)
    accum, solved_local = lax.fori_loop(0, level_count, home_level, (accum, solved_local))
    return (half_local[:, None], solved_local[:, None])


def solution(mesh):
    return jax.shard_map(
        per_device,
        mesh=mesh,
        in_specs=(
            P(None, "chain", None, None),
            P(None, "chain", "col"),
            P(None, "chain", "col", None, None),
            P(None, "chain", None, None),
            P(),
        ),
        out_specs=(P(None, "chain", None, None), P(None, "chain", None, None)),
        check_vma=False,
    )
```

profile of v0, /device:TPU:0, one launch (start us, length us, event | category | flops | bytes accessed | tf_op | source)
XLA Modules:
  0.0 617.3 jit_solution(10101479652952594900)
XLA Ops:
  1.1 1.3 reduce.3
  4.0 7.3 %all-to-all-start = ((s32[8,3,2]{1,2,0:T(2,128)}), s32[8,3,2]{1,2,0:T(2,128)S(1)}, u32[]{:S(2)}, u32[]{:S(2)}) async-start(s32[8,3,2]{1,2,0:T(2,128)} %copy.16), calls=%async_computation | async-start | bytes 16384 | tf_op jit(solution)/shard_map/all_to_all | solution.py:87
  11.3 0.8 reduce-window.8
  12.1 0.8 copy.14
  14.0 1.8 fusion.43
  15.9 1.0 copy.21
  17.0 0.9 all-to-all-done
  17.8 5.3 all-to-all-start.1
  23.2 314.8 %while.35 = (s32[]{:T(128)}, bf16[40,32,128]{2,1,0:T(8,128)(2,1)S(1)}, bf16[4,32,128]{2,1,0:T(8,128)(2,1)S(1)}, s32[4]{0:T(128)S(1)}, bf16[4,32,128]{2,1,0:T(8,1...) while((s32[]{:T(128)}, ...), condition=%wide.region_7.8_spmd.clone, body=%wide.region_3.7_spmd.clone.sunk | while | flops 7424167 | bytes 878571 | solution.py:63
  23.8 0.7 fusion.82
  28.3 1.1 convolution_bitcast_fusion.2
  29.5 10.4 %psum.30 = f32[32,128]{1,0:T(8,128)S(1)} all-reduce(f32[32,128]{1,0:T(8,128)S(1)} %convolution_bitcast_fusion.2), channel_id=1, replica_groups=mesh['chain'=8,'col'=4] {'col'}, use_global_device_ids=true, to_apply=%region_6.6 | all-reduce | flops 4096 | bytes 32768 | tf_op jit(solution)/shard_map/while/body/eval_jaxpr/psum | solution.py:48
  39.9 1.5 fusion.84
  41.4 31.1 %all-gather.6 = bf16[256,128]{1,0:T(8,128)(2,1)S(1)} all-gather(bf16[32,128]{1,0:T(8,128)(2,1)S(1)} %fusion.84), channel_id=2, replica_groups=mesh['chain'=8,'col'=4] {'chain'}, dimensions={0}, use_global_device_ids=true | all-gather | bytes 73728 | tf_op jit(solution)/shard_map/while/body/eval_jaxpr/all_gather | solution.py:54
  77.0 0.7 fusion.82
  81.5 1.1 convolution_bitcast_fusion.2
  82.6 10.1 %psum.30 = f32[32,128]{1,0:T(8,128)S(1)} all-reduce(f32[32,128]{1,0:T(8,128)S(1)} %convolution_bitcast_fusion.2), channel_id=1, replica_groups=mesh['chain'=8,'col'=4] {'col'}, use_global_device_ids=true, to_apply=%region_6.6 | all-reduce | flops 4096 | bytes 32768 | tf_op jit(solution)/shard_map/while/body/eval_jaxpr/psum | solution.py:48
  92.8 1.5 fusion.84
  94.2 30.6 %all-gather.6 = bf16[256,128]{1,0:T(8,128)(2,1)S(1)} all-gather(bf16[32,128]{1,0:T(8,128)(2,1)S(1)} %fusion.84), channel_id=2, replica_groups=mesh['chain'=8,'col'=4] {'chain'}, dimensions={0}, use_global_device_ids=true | all-gather | bytes 73728 | tf_op jit(solution)/shard_map/while/body/eval_jaxpr/all_gather | solution.py:54
  129.3 0.7 fusion.82
  133.8 1.1 convolution_bitcast_fusion.2
  135.0 10.1 %psum.30 = f32[32,128]{1,0:T(8,128)S(1)} all-reduce(f32[32,128]{1,0:T(8,128)S(1)} %convolution_bitcast_fusion.2), channel_id=1, replica_groups=mesh['chain'=8,'col'=4] {'col'}, use_global_device_ids=true, to_apply=%region_6.6 | all-reduce | flops 4096 | bytes 32768 | tf_op jit(solution)/shard_map/while/body/eval_jaxpr/psum | solution.py:48
  145.1 1.5 fusion.84
  146.6 30.6 %all-gather.6 = bf16[256,128]{1,0:T(8,128)(2,1)S(1)} all-gather(bf16[32,128]{1,0:T(8,128)(2,1)S(1)} %fusion.84), channel_id=2, replica_groups=mesh['chain'=8,'col'=4] {'chain'}, dimensions={0}, use_global_device_ids=true | all-gather | bytes 73728 | tf_op jit(solution)/shard_map/while/body/eval_jaxpr/all_gather | solution.py:54
  181.6 0.7 fusion.82
  186.2 1.1 convolution_bitcast_fusion.2
  187.3 10.1 %psum.30 = f32[32,128]{1,0:T(8,128)S(1)} all-reduce(f32[32,128]{1,0:T(8,128)S(1)} %convolution_bitcast_fusion.2), channel_id=1, replica_groups=mesh['chain'=8,'col'=4] {'col'}, use_global_device_ids=true, to_apply=%region_6.6 | all-reduce | flops 4096 | bytes 32768 | tf_op jit(solution)/shard_map/while/body/eval_jaxpr/psum | solution.py:48
  197.4 1.5 fusion.84
  198.9 30.6 %all-gather.6 = bf16[256,128]{1,0:T(8,128)(2,1)S(1)} all-gather(bf16[32,128]{1,0:T(8,128)(2,1)S(1)} %fusion.84), channel_id=2, replica_groups=mesh['chain'=8,'col'=4] {'chain'}, dimensions={0}, use_global_device_ids=true | all-gather | bytes 73728 | tf_op jit(solution)/shard_map/while/body/eval_jaxpr/all_gather | solution.py:54
  234.0 0.7 fusion.82
  238.5 1.1 convolution_bitcast_fusion.2
  239.6 10.1 %psum.30 = f32[32,128]{1,0:T(8,128)S(1)} all-reduce(f32[32,128]{1,0:T(8,128)S(1)} %convolution_bitcast_fusion.2), channel_id=1, replica_groups=mesh['chain'=8,'col'=4] {'col'}, use_global_device_ids=true, to_apply=%region_6.6 | all-reduce | flops 4096 | bytes 32768 | tf_op jit(solution)/shard_map/while/body/eval_jaxpr/psum | solution.py:48
  249.8 1.5 fusion.84
  251.2 30.6 %all-gather.6 = bf16[256,128]{1,0:T(8,128)(2,1)S(1)} all-gather(bf16[32,128]{1,0:T(8,128)(2,1)S(1)} %fusion.84), channel_id=2, replica_groups=mesh['chain'=8,'col'=4] {'chain'}, dimensions={0}, use_global_device_ids=true | all-gather | bytes 73728 | tf_op jit(solution)/shard_map/while/body/eval_jaxpr/all_gather | solution.py:54
  286.3 0.7 fusion.82
  290.8 1.1 convolution_bitcast_fusion.2
  291.9 10.1 %psum.30 = f32[32,128]{1,0:T(8,128)S(1)} all-reduce(f32[32,128]{1,0:T(8,128)S(1)} %convolution_bitcast_fusion.2), channel_id=1, replica_groups=mesh['chain'=8,'col'=4] {'col'}, use_global_device_ids=true, to_apply=%region_6.6 | all-reduce | flops 4096 | bytes 32768 | tf_op jit(solution)/shard_map/while/body/eval_jaxpr/psum | solution.py:48
  302.1 1.5 fusion.84
  303.6 30.6 %all-gather.6 = bf16[256,128]{1,0:T(8,128)(2,1)S(1)} all-gather(bf16[32,128]{1,0:T(8,128)(2,1)S(1)} %fusion.84), channel_id=2, replica_groups=mesh['chain'=8,'col'=4] {'chain'}, dimensions={0}, use_global_device_ids=true | all-gather | bytes 73728 | tf_op jit(solution)/shard_map/while/body/eval_jaxpr/all_gather | solution.py:54
  338.2 278.4 %while.36 = (s32[]{:T(128)}, f32[4,32,128]{2,0,1:T(4,128)S(1)}, bf16[4,32,128]{2,1,0:T(8,128)(2,1)S(1)}, s32[24]{0:T(128)S(1)}, s32[24]{0:T(128)S(1)}, /*index=5...) while((s32[]{:T(128)}, f32[4,32,128]{2,0,1:T(4,128)S(1)}, ...), condition=%wide.region_18.19_spmd.clone.clone, body=%wide.region_14.18_spmd.clone.clone.sunk | while | flops 31024460 | bytes 2709372 | solution.py:128
  338.9 0.7 fusion.93
  341.7 10.1 %psum.31 = f32[32,128]{1,0:T(8,128)S(1)} all-reduce(f32[32,128]{1,0:T(8,128)S(1)} %bitcast.150), channel_id=1, replica_groups=mesh['chain'=8,'col'=4] {'col'}, use_global_device_ids=true, to_apply=%region_17.17 | all-reduce | flops 4096 | bytes 32768 | tf_op jit(solution)/shard_map/while/body/eval_jaxpr/psum | solution.py:104
  351.8 0.8 fusion.94
  352.6 30.5 %all-gather.7 = bf16[256,128]{1,0:T(8,128)(2,1)S(1)} all-gather(bf16[32,128]{1,0:T(8,128)(2,1)S(1)} %fusion.94), channel_id=3, replica_groups=mesh['chain'=8,'col'=4] {'chain'}, dimensions={0}, use_global_device_ids=true | all-gather | bytes 73728 | tf_op jit(solution)/shard_map/while/body/eval_jaxpr/all_gather | solution.py:111
  385.3 0.7 fusion.93
  388.1 10.1 %psum.31 = f32[32,128]{1,0:T(8,128)S(1)} all-reduce(f32[32,128]{1,0:T(8,128)S(1)} %bitcast.150), channel_id=1, replica_groups=mesh['chain'=8,'col'=4] {'col'}, use_global_device_ids=true, to_apply=%region_17.17 | all-reduce | flops 4096 | bytes 32768 | tf_op jit(solution)/shard_map/while/body/eval_jaxpr/psum | solution.py:104
  398.2 0.8 fusion.94
  399.0 30.5 %all-gather.7 = bf16[256,128]{1,0:T(8,128)(2,1)S(1)} all-gather(bf16[32,128]{1,0:T(8,128)(2,1)S(1)} %fusion.94), channel_id=3, replica_groups=mesh['chain'=8,'col'=4] {'chain'}, dimensions={0}, use_global_device_ids=true | all-gather | bytes 73728 | tf_op jit(solution)/shard_map/while/body/eval_jaxpr/all_gather | solution.py:111
  431.7 0.7 fusion.93
  434.5 10.1 %psum.31 = f32[32,128]{1,0:T(8,128)S(1)} all-reduce(f32[32,128]{1,0:T(8,128)S(1)} %bitcast.150), channel_id=1, replica_groups=mesh['chain'=8,'col'=4] {'col'}, use_global_device_ids=true, to_apply=%region_17.17 | all-reduce | flops 4096 | bytes 32768 | tf_op jit(solution)/shard_map/while/body/eval_jaxpr/psum | solution.py:104
  444.6 0.8 fusion.94
  445.4 30.5 %all-gather.7 = bf16[256,128]{1,0:T(8,128)(2,1)S(1)} all-gather(bf16[32,128]{1,0:T(8,128)(2,1)S(1)} %fusion.94), channel_id=3, replica_groups=mesh['chain'=8,'col'=4] {'chain'}, dimensions={0}, use_global_device_ids=true | all-gather | bytes 73728 | tf_op jit(solution)/shard_map/while/body/eval_jaxpr/all_gather | solution.py:111
  478.1 0.7 fusion.93
  480.9 10.1 %psum.31 = f32[32,128]{1,0:T(8,128)S(1)} all-reduce(f32[32,128]{1,0:T(8,128)S(1)} %bitcast.150), channel_id=1, replica_groups=mesh['chain'=8,'col'=4] {'col'}, use_global_device_ids=true, to_apply=%region_17.17 | all-reduce | flops 4096 | bytes 32768 | tf_op jit(solution)/shard_map/while/body/eval_jaxpr/psum | solution.py:104
  491.0 0.8 fusion.94
  491.8 30.5 %all-gather.7 = bf16[256,128]{1,0:T(8,128)(2,1)S(1)} all-gather(bf16[32,128]{1,0:T(8,128)(2,1)S(1)} %fusion.94), channel_id=3, replica_groups=mesh['chain'=8,'col'=4] {'chain'}, dimensions={0}, use_global_device_ids=true | all-gather | bytes 73728 | tf_op jit(solution)/shard_map/while/body/eval_jaxpr/all_gather | solution.py:111
  524.5 0.7 fusion.93
  527.3 10.1 %psum.31 = f32[32,128]{1,0:T(8,128)S(1)} all-reduce(f32[32,128]{1,0:T(8,128)S(1)} %bitcast.150), channel_id=1, replica_groups=mesh['chain'=8,'col'=4] {'col'}, use_global_device_ids=true, to_apply=%region_17.17 | all-reduce | flops 4096 | bytes 32768 | tf_op jit(solution)/shard_map/while/body/eval_jaxpr/psum | solution.py:104
  537.4 0.8 fusion.94
  538.2 30.5 %all-gather.7 = bf16[256,128]{1,0:T(8,128)(2,1)S(1)} all-gather(bf16[32,128]{1,0:T(8,128)(2,1)S(1)} %fusion.94), channel_id=3, replica_groups=mesh['chain'=8,'col'=4] {'chain'}, dimensions={0}, use_global_device_ids=true | all-gather | bytes 73728 | tf_op jit(solution)/shard_map/while/body/eval_jaxpr/all_gather | solution.py:111
  570.9 0.7 fusion.93
  573.7 10.1 %psum.31 = f32[32,128]{1,0:T(8,128)S(1)} all-reduce(f32[32,128]{1,0:T(8,128)S(1)} %bitcast.150), channel_id=1, replica_groups=mesh['chain'=8,'col'=4] {'col'}, use_global_device_ids=true, to_apply=%region_17.17 | all-reduce | flops 4096 | bytes 32768 | tf_op jit(solution)/shard_map/while/body/eval_jaxpr/psum | solution.py:104
  583.8 0.8 fusion.94
  584.6 30.5 %all-gather.7 = bf16[256,128]{1,0:T(8,128)(2,1)S(1)} all-gather(bf16[32,128]{1,0:T(8,128)(2,1)S(1)} %fusion.94), channel_id=3, replica_groups=mesh['chain'=8,'col'=4] {'chain'}, dimensions={0}, use_global_device_ids=true | all-gather | bytes 73728 | tf_op jit(solution)/shard_map/while/body/eval_jaxpr/all_gather | solution.py:111
  (165 shorter events, 43.7 us)
Async XLA Ops:
  4.0 13.8 %all-to-all-start = ((s32[8,3,2]{1,2,0:T(2,128)}), s32[8,3,2]{1,2,0:T(2,128)S(1)}, u32[]{:S(2)}, u32[]{:S(2)}) async-start(s32[8,3,2]{1,2,0:T(2,128)} %copy.16), calls=%async_computation | async-start | bytes 16384 | tf_op jit(solution)/shard_map/all_to_all | solution.py:87
  17.8 5.3 copy-start.2
  17.8 320.4 %all-to-all-start.1 = ((bf16[8,3,128,128]{3,2,1,0:T(8,128)(2,1)}), bf16[8,3,128,128]{3,2,1,0:T(8,128)(2,1)S(1)}, u32[]{:S(2)}, u32[]{:S(2)}) async-start(bf16[8,3,128,128]{3,2,1,0:T(8,128)(2,1)} %bitcast.42), calls=%async_computation.1 | async-start | bytes 1572864 | tf_op jit(solution)/shard_map/all_to_all | solution.py:86
  616.6 0.6 copy-start
  616.6 0.6 copy-start.1
where the time goes:
time: 619 us; the launch traced here: 617 us
  blocking collectives  489 us (79%)
  loops' own time  36 us (6%)
  other arithmetic  33.2 us (5%)
  matrix products  26.7 us (4%)
  local copies, waits for them, and re-layouts  18.2 us (3%)
  starting transfers between devices  12.6 us (2%)
    all_gather x6, blocking collectives, forward_level(): front = lax.all_gather(segment[None], 'chain', axis=0, tiled=True)  184 us
    all_gather x6, blocking collectives, home_level(): front = lax.all_gather(segment[None], 'chain', axis=0, tiled=True)  183 us
    psum x6, blocking collectives, forward_level(): summed = lax.psum(partial_value, 'col')  61.1 us
    psum x6, blocking collectives, home_level(): summed = lax.psum(accum[own_slot], 'col')  60.7 us
    another operation x1, loops' own time, per_device(): lax.fori_loop(0, level_count, forward_level, (store, half_local))  23.3 us
    another operation x1, loops' own time, per_device(): lax.fori_loop(0, level_count, home_level, (accum, solved_local))  12.7 us
  transfers between devices with their start and end apart: 2, of which 1 were waited for; matrix products, arithmetic and copies ran while one was open for 8% of the time, Pallas kernels for 0%

commit v1 on v0

--- a/solution.py
+++ b/solution.py
@@ -2,6 +2,18 @@
 import jax.numpy as jnp
 from jax import lax
 from jax.sharding import PartitionSpec as P
+
+
+def gather_by_bits(x, axis, dim):
+    ways, here = (lax.axis_size(axis), lax.axis_index(axis))
+    grown, reach = (x, 1)
+    while reach < ways:
+        theirs = lax.ppermute(grown, axis, [(d, d ^ reach) for d in range(ways)])
+        mine_first = jnp.concatenate([grown, theirs], axis=dim)
+        theirs_first = jnp.concatenate([theirs, grown], axis=dim)
+        grown = jnp.where(here & reach == 0, mine_first, theirs_first)
+        reach = 2 * reach
+    return grown
 
 
 def level_index(positions, ends):
@@ -108,7 +120,7 @@
         )
         segment = jnp.where(is_live, segment, jnp.zeros((), jnp.bfloat16))
         solved_now = jnp.where(picked[:, None, None], segment[None], solved_now)
-        front = lax.all_gather(segment[None], "chain", axis=0, tiled=True)
+        front = gather_by_bits(segment[None], "chain", 0)
         active = home_keep & (source_level == level)
         incoming = front[source_lane]
         terms = jnp.einsum(

time: 619 us -> 510 us (0.82)
  blocking collectives: 489 us -> 306 us
  waiting for transfers between devices: 0.85 us -> 57.5 us
  starting transfers between devices: 12.6 us -> 29.2 us
    all_gather x6 -> x0, blocking collectives: 183 us -> none  [home_level(): front = lax.all_gather(segment[None], 'chain', axis=0, tiled=True)]
    ppermute x0 -> x18, waiting for transfers between devices: none -> 56.7 us  [gather_by_bits(): theirs = lax.ppermute(grown, axis, [(d, d ^ reach) for d in range(ways)])]
    ppermute x0 -> x18, starting transfers between devices: none -> 16.6 us  [gather_by_bits(): theirs = lax.ppermute(grown, axis, [(d, d ^ reach) for d in range(ways)])]
  transfers between devices with their start and end apart: 2 -> 20, of which waited for: 1 -> 19; matrix products, arithmetic and copies ran while one was open for 8% -> 10% of each run, Pallas kernels for 0% -> 0%
where the time goes in v1:
time: 510 us; the launch traced here: 508 us
  blocking collectives  306 us (60%)
  waiting for transfers between devices  57.5 us (11%)
  loops' own time  36.2 us (7%)
  other arithmetic  33.3 us (7%)
  starting transfers between devices  29.2 us (6%)
  matrix products  26.7 us (5%)
  local copies, waits for them, and re-layouts  18.2 us (4%)
    all_gather x6, blocking collectives, forward_level(): front = lax.all_gather(segment[None], 'chain', axis=0, tiled=True)  184 us
    psum x6, blocking collectives, forward_level(): summed = lax.psum(partial_value, 'col')  61.1 us
    psum x6, blocking collectives, home_level(): summed = lax.psum(accum[own_slot], 'col')  60.7 us
    ppermute x18, waiting for transfers between devices, gather_by_bits(): theirs = lax.ppermute(grown, axis, [(d, d ^ reach) for d in range(ways)])  56.7 us
    another operation x1, loops' own time, per_device(): lax.fori_loop(0, level_count, forward_level, (store, half_local))  23.3 us
    ppermute x18, starting transfers between devices, gather_by_bits(): theirs = lax.ppermute(grown, axis, [(d, d ^ reach) for d in range(ways)])  16.6 us
    another operation x1, loops' own time, per_device(): lax.fori_loop(0, level_count, home_level, (accum, solved_local))  12.9 us
  transfers between devices with their start and end apart: 20, of which 19 were waited for; matrix products, arithmetic and copies ran while one was open for 10% of the time, Pallas kernels for 0%

profile of v1, /device:TPU:0, one launch (start us, length us, event | category | flops | bytes accessed | tf_op | source)
XLA Modules:
  0.0 507.6 jit_solution(1890398373732575165)
XLA Ops:
  1.1 1.3 reduce.3
  4.0 7.3 %all-to-all-start = ((s32[8,3,2]{1,2,0:T(2,128)}), s32[8,3,2]{1,2,0:T(2,128)S(1)}, u32[]{:S(2)}, u32[]{:S(2)}) async-start(s32[8,3,2]{1,2,0:T(2,128)} %copy.16), calls=%async_computation | async-start | bytes 16384 | tf_op jit(solution)/shard_map/all_to_all | solution.py:99
  14.0 1.8 fusion.43
  17.8 5.3 %all-to-all-start.1 = ((bf16[8,3,128,128]{3,2,1,0:T(8,128)(2,1)}), bf16[8,3,128,128]{3,2,1,0:T(8,128)(2,1)S(1)}, u32[]{:S(2)}, u32[]{:S(2)}) async-start(bf16[8,3,128,128]{3,2,1,0:T(8,128)(2,1)} %bitcast.42), calls=%async_computation.1 | async-start | bytes 1572864 | tf_op jit(solution)/shard_map/all_to_all | solution.py:98
  23.2 314.8 %while.35 = (s32[]{:T(128)}, bf16[40,32,128]{2,1,0:T(8,128)(2,1)S(1)}, bf16[4,32,128]{2,1,0:T(8,128)(2,1)S(1)}, s32[4]{0:T(128)S(1)}, bf16[4,32,128]{2,1,0:T(8,1...) while((s32[]{:T(128)}, ...), condition=%wide.region_7.8_spmd.clone, body=%wide.region_3.7_spmd.clone.sunk | while | flops 7424167 | bytes 878571 | solution.py:75
  28.3 1.1 convolution_bitcast_fusion.2
  29.5 10.4 %psum.30 = f32[32,128]{1,0:T(8,128)S(1)} all-reduce(f32[32,128]{1,0:T(8,128)S(1)} %convolution_bitcast_fusion.2), channel_id=1, replica_groups=mesh['chain'=8,'col'=4] {'col'}, use_global_device_ids=true, to_apply=%region_6.6 | all-reduce | flops 4096 | bytes 32768 | tf_op jit(solution)/shard_map/while/body/eval_jaxpr/psum | solution.py:60
  39.9 1.5 fusion.84
  41.4 31.1 %all-gather.3 = bf16[256,128]{1,0:T(8,128)(2,1)S(1)} all-gather(bf16[32,128]{1,0:T(8,128)(2,1)S(1)} %fusion.84), channel_id=2, replica_groups=mesh['chain'=8,'col'=4] {'chain'}, dimensions={0}, use_global_device_ids=true | all-gather | bytes 73728 | tf_op jit(solution)/shard_map/while/body/eval_jaxpr/all_gather | solution.py:66
  81.5 1.1 convolution_bitcast_fusion.2
  82.6 10.1 %psum.30 = f32[32,128]{1,0:T(8,128)S(1)} all-reduce(f32[32,128]{1,0:T(8,128)S(1)} %convolution_bitcast_fusion.2), channel_id=1, replica_groups=mesh['chain'=8,'col'=4] {'col'}, use_global_device_ids=true, to_apply=%region_6.6 | all-reduce | flops 4096 | bytes 32768 | tf_op jit(solution)/shard_map/while/body/eval_jaxpr/psum | solution.py:60
  92.8 1.5 fusion.84
  94.2 30.6 %all-gather.3 = bf16[256,128]{1,0:T(8,128)(2,1)S(1)} all-gather(bf16[32,128]{1,0:T(8,128)(2,1)S(1)} %fusion.84), channel_id=2, replica_groups=mesh['chain'=8,'col'=4] {'chain'}, dimensions={0}, use_global_device_ids=true | all-gather | bytes 73728 | tf_op jit(solution)/shard_map/while/body/eval_jaxpr/all_gather | solution.py:66
  133.8 1.1 convolution_bitcast_fusion.2
  135.0 10.1 %psum.30 = f32[32,128]{1,0:T(8,128)S(1)} all-reduce(f32[32,128]{1,0:T(8,128)S(1)} %convolution_bitcast_fusion.2), channel_id=1, replica_groups=mesh['chain'=8,'col'=4] {'col'}, use_global_device_ids=true, to_apply=%region_6.6 | all-reduce | flops 4096 | bytes 32768 | tf_op jit(solution)/shard_map/while/body/eval_jaxpr/psum | solution.py:60
  145.1 1.5 fusion.84
  146.6 30.6 %all-gather.3 = bf16[256,128]{1,0:T(8,128)(2,1)S(1)} all-gather(bf16[32,128]{1,0:T(8,128)(2,1)S(1)} %fusion.84), channel_id=2, replica_groups=mesh['chain'=8,'col'=4] {'chain'}, dimensions={0}, use_global_device_ids=true | all-gather | bytes 73728 | tf_op jit(solution)/shard_map/while/body/eval_jaxpr/all_gather | solution.py:66
  187.3 10.1 %psum.30 = f32[32,128]{1,0:T(8,128)S(1)} all-reduce(f32[32,128]{1,0:T(8,128)S(1)} %convolution_bitcast_fusion.2), channel_id=1, replica_groups=mesh['chain'=8,'col'=4] {'col'}, use_global_device_ids=true, to_apply=%region_6.6 | all-reduce | flops 4096 | bytes 32768 | tf_op jit(solution)/shard_map/while/body/eval_jaxpr/psum | solution.py:60
  197.4 1.5 fusion.84
  198.9 30.6 %all-gather.3 = bf16[256,128]{1,0:T(8,128)(2,1)S(1)} all-gather(bf16[32,128]{1,0:T(8,128)(2,1)S(1)} %fusion.84), channel_id=2, replica_groups=mesh['chain'=8,'col'=4] {'chain'}, dimensions={0}, use_global_device_ids=true | all-gather | bytes 73728 | tf_op jit(solution)/shard_map/while/body/eval_jaxpr/all_gather | solution.py:66
  239.6 10.1 %psum.30 = f32[32,128]{1,0:T(8,128)S(1)} all-reduce(f32[32,128]{1,0:T(8,128)S(1)} %convolution_bitcast_fusion.2), channel_id=1, replica_groups=mesh['chain'=8,'col'=4] {'col'}, use_global_device_ids=true, to_apply=%region_6.6 | all-reduce | flops 4096 | bytes 32768 | tf_op jit(solution)/shard_map/while/body/eval_jaxpr/psum | solution.py:60
  249.8 1.5 fusion.84
  251.2 30.6 %all-gather.3 = bf16[256,128]{1,0:T(8,128)(2,1)S(1)} all-gather(bf16[32,128]{1,0:T(8,128)(2,1)S(1)} %fusion.84), channel_id=2, replica_groups=mesh['chain'=8,'col'=4] {'chain'}, dimensions={0}, use_global_device_ids=true | all-gather | bytes 73728 | tf_op jit(solution)/shard_map/while/body/eval_jaxpr/all_gather | solution.py:66
  290.8 1.1 convolution_bitcast_fusion.2
  291.9 10.1 %psum.30 = f32[32,128]{1,0:T(8,128)S(1)} all-reduce(f32[32,128]{1,0:T(8,128)S(1)} %convolution_bitcast_fusion.2), channel_id=1, replica_groups=mesh['chain'=8,'col'=4] {'col'}, use_global_device_ids=true, to_apply=%region_6.6 | all-reduce | flops 4096 | bytes 32768 | tf_op jit(solution)/shard_map/while/body/eval_jaxpr/psum | solution.py:60
  302.1 1.5 fusion.84
  303.6 30.6 %all-gather.3 = bf16[256,128]{1,0:T(8,128)(2,1)S(1)} all-gather(bf16[32,128]{1,0:T(8,128)(2,1)S(1)} %fusion.84), channel_id=2, replica_groups=mesh['chain'=8,'col'=4] {'chain'}, dimensions={0}, use_global_device_ids=true | all-gather | bytes 73728 | tf_op jit(solution)/shard_map/while/body/eval_jaxpr/all_gather | solution.py:66
  338.2 168.8 %while.36 = (s32[]{:T(128)}, f32[4,32,128]{2,0,1:T(4,128)S(1)}, bf16[4,32,128]{2,1,0:T(8,128)(2,1)S(1)}, s32[24]{0:T(128)S(1)}, s32[24]{0:T(128)S(1)}, /*index=5...) while((s32[]{:T(128)}, f32[4,32,128]{2,0,1:T(4,128)S(1)}, ...), condition=%wide.region_18.19_spmd.clone.clone, body=%wide.region_14.18_spmd.clone.clone.sunk | while | flops 31196500 | bytes 3094638 | solution.py:140
  341.7 10.1 %psum.31 = f32[32,128]{1,0:T(8,128)S(1)} all-reduce(f32[32,128]{1,0:T(8,128)S(1)} %bitcast.151), channel_id=1, replica_groups=mesh['chain'=8,'col'=4] {'col'}, use_global_device_ids=true, to_apply=%region_17.17 | all-reduce | flops 4096 | bytes 32768 | tf_op jit(solution)/shard_map/while/body/eval_jaxpr/psum | solution.py:116
  352.6 1.5 collective-permute-start
  354.2 2.1 collective-permute-done
  356.3 3.7 collective-permute-done.1
  360.0 1.3 collective-permute-start.2
  361.3 3.7 collective-permute-done.2
  369.9 10.1 %psum.31 = f32[32,128]{1,0:T(8,128)S(1)} all-reduce(f32[32,128]{1,0:T(8,128)S(1)} %bitcast.151), channel_id=1, replica_groups=mesh['chain'=8,'col'=4] {'col'}, use_global_device_ids=true, to_apply=%region_17.17 | all-reduce | flops 4096 | bytes 32768 | tf_op jit(solution)/shard_map/while/body/eval_jaxpr/psum | solution.py:116
  380.8 1.4 collective-permute-start
  382.3 2.2 collective-permute-done
  384.7 3.5 collective-permute-done.1
  388.2 1.2 collective-permute-start.2
  389.4 3.7 collective-permute-done.2
  398.0 10.1 %psum.31 = f32[32,128]{1,0:T(8,128)S(1)} all-reduce(f32[32,128]{1,0:T(8,128)S(1)} %bitcast.151), channel_id=1, replica_groups=mesh['chain'=8,'col'=4] {'col'}, use_global_device_ids=true, to_apply=%region_17.17 | all-reduce | flops 4096 | bytes 32768 | tf_op jit(solution)/shard_map/while/body/eval_jaxpr/psum | solution.py:116
  408.9 1.4 collective-permute-start
  410.4 2.2 collective-permute-done
  412.8 3.5 collective-permute-done.1
  416.3 1.2 collective-permute-start.2
  417.5 3.7 collective-permute-done.2
  426.1 10.1 %psum.31 = f32[32,128]{1,0:T(8,128)S(1)} all-reduce(f32[32,128]{1,0:T(8,128)S(1)} %bitcast.151), channel_id=1, replica_groups=mesh['chain'=8,'col'=4] {'col'}, use_global_device_ids=true, to_apply=%region_17.17 | all-reduce | flops 4096 | bytes 32768 | tf_op jit(solution)/shard_map/while/body/eval_jaxpr/psum | solution.py:116
  437.0 1.4 collective-permute-start
  438.4 2.2 collective-permute-done
  440.9 3.5 collective-permute-done.1
  444.4 1.1 collective-permute-start.2
  445.6 3.7 collective-permute-done.2
  454.2 10.1 %psum.31 = f32[32,128]{1,0:T(8,128)S(1)} all-reduce(f32[32,128]{1,0:T(8,128)S(1)} %bitcast.151), channel_id=1, replica_groups=mesh['chain'=8,'col'=4] {'col'}, use_global_device_ids=true, to_apply=%region_17.17 | all-reduce | flops 4096 | bytes 32768 | tf_op jit(solution)/shard_map/while/body/eval_jaxpr/psum | solution.py:116
  465.1 1.4 collective-permute-start
  466.5 2.2 collective-permute-done
  469.0 3.5 collective-permute-done.1
  472.5 1.1 collective-permute-start.2
  473.6 3.7 collective-permute-done.2
  482.3 10.1 %psum.31 = f32[32,128]{1,0:T(8,128)S(1)} all-reduce(f32[32,128]{1,0:T(8,128)S(1)} %bitcast.151), channel_id=1, replica_groups=mesh['chain'=8,'col'=4] {'col'}, use_global_device_ids=true, to_apply=%region_17.17 | all-reduce | flops 4096 | bytes 32768 | tf_op jit(solution)/shard_map/while/body/eval_jaxpr/psum | solution.py:116
  493.2 1.3 collective-permute-start
  494.6 2.2 collective-permute-done
  497.2 3.4 collective-permute-done.1
  500.6 1.2 collective-permute-start.2
  501.8 3.8 collective-permute-done.2
  (213 shorter events, 63.9 us)
Async XLA Ops:
  4.0 13.8 %all-to-all-start = ((s32[8,3,2]{1,2,0:T(2,128)}), s32[8,3,2]{1,2,0:T(2,128)S(1)}, u32[]{:S(2)}, u32[]{:S(2)}) async-start(s32[8,3,2]{1,2,0:T(2,128)} %copy.16), calls=%async_computation | async-start | bytes 16384 | tf_op jit(solution)/shard_map/all_to_all | solution.py:99
  17.8 5.3 %copy-start.2 = (bf16[4,1,128,128]{3,2,1,0:T(8,128)(2,1)S(1)}, bf16[4,1,128,128]{3,2,1,0:T(8,128)(2,1)}, u32[]{:S(2)}) copy-start(bf16[4,1,128,128]{3,2,1,0:T(8,128)(2,1)} %param.12) | copy-start | bytes 393220
  17.8 320.4 %all-to-all-start.1 = ((bf16[8,3,128,128]{3,2,1,0:T(8,128)(2,1)}), bf16[8,3,128,128]{3,2,1,0:T(8,128)(2,1)S(1)}, u32[]{:S(2)}, u32[]{:S(2)}) async-start(bf16[8,3,128,128]{3,2,1,0:T(8,128)(2,1)} %bitcast.42), calls=%async_computation.1 | async-start | bytes 1572864 | tf_op jit(solution)/shard_map/all_to_all | solution.py:98
  352.6 3.7 collective-permute-start
  356.3 3.7 collective-permute-start.1
  360.0 5.0 collective-permute-start.2
  380.8 3.7 collective-permute-start
  384.5 3.7 collective-permute-start.1
  388.2 4.9 collective-permute-start.2
  408.9 3.7 collective-permute-start
  412.6 3.7 collective-permute-start.1
  416.3 4.9 collective-permute-start.2
  437.0 3.7 collective-permute-start
  440.7 3.7 collective-permute-start.1
  444.4 4.9 collective-permute-start.2
  465.1 3.7 collective-permute-start
  468.7 3.7 collective-permute-start.1
  472.5 4.9 collective-permute-start.2
  493.2 3.7 collective-permute-start
  496.8 3.7 collective-permute-start.1
  500.6 5.0 collective-permute-start.2
  507.0 0.6 copy-start
  507.0 0.6 copy-start.1
